TPU v7x, 32 devices: a whole 2x2x4 slice. The times are simulated.
32 devices in a mesh: batch: 2 (over y), freq: 8 (over z, x), elem: 2 (over core).
Axes of the slice: x: 2, y: 2, z: 4, core: 2. Of those that a mesh axis runs over, the one named last changes fastest.
Arguments:
- flaw_cells: int32 [512], P('batch'), parts along dimension 0, may hold values from 0 to 255, each once
- flaw_blocks: int32 [16], P('batch'), parts along dimension 0, may hold values from 0 to 7, each once
- element_channel: int32 [256], P('elem'), may hold values from 0 to 255, each once
- focal_delay: float32 [256, 256], replicated, may hold values from 0 to 64
- beam_field: bfloat16 [128, 2, 256, 256], P('freq', None, 'elem'), may hold values from -0.125 to 0.125
- flaw_size: float32 [4, 128], P('batch'), parts along dimension 0, may hold values from 0.5 to 4
- flaw_slope: float32 [4, 128], P('batch'), parts along dimension 0, may hold values from 0.2 to 1
- noise_level: float32 [4, 128], P(('batch', 'elem'), 'freq'), parts along dimension 0, may hold values from 0.5 to 5
Outputs:
- flaw_peak: float32 [4, 128], P(('batch', 'elem'), 'freq'), parts along dimension 0
- detection: float32 [4, 128], P(('batch', 'elem'), 'freq'), parts along dimension 0
There are 2 independent parts, one for each index of `batch`. A program takes and returns all parts, laid end to end along the dimension named above; an argument that names none is the same for every part. Nothing has to cross between parts.
Inputs may be any that keep to these rules, and one draw needn't show every extreme that they name: `flaw_cells`: every site holds exactly one flaw. `flaw_blocks`: every scan block belongs to exactly one flaw group. `element_channel`: every channel drives exactly one element.
All inputs are finite; a program needn't handle non-finite values.
Results may differ from a plain program's by a relative error of at most 0.0011.
Values may be sent and summed in bfloat16 or wider, within the bound.
A program may use at most 64 MiB of HBM per device.

v0:
```python
import math

import jax
import jax.numpy as jnp
from jax import lax
from jax.sharding import PartitionSpec as P

W_DEV = 16
FG = 128
NB = 4
SB = 32
T_CAP = 1024


EDGE = 0.6
STEEP = 3.0
EPS = 1e-05


def kirchhoff(angular, flaw_size, flaw_slope):
    angles = angular[None, :, None] * (2.0 * flaw_size * flaw_slope)[:, None, :]
    real_part = flaw_size[:, None, :] * (1.0 + EDGE) * jnp.cos(angles)
    imag_part = flaw_size[:, None, :] * (EDGE - 1.0) * jnp.sin(angles)
    return (real_part, imag_part)


def focal_law(angular, delays):
    phases = angular[:, None, None, None] * delays[None]
    return jnp.concatenate([jnp.cos(phases), -jnp.sin(phases)], axis=-1).astype(jnp.bfloat16)


def field_matrix(fields):
    real_part = fields[:, 0]
    imag_part = fields[:, 1]
    upper_rows = jnp.concatenate([real_part, imag_part], axis=-1)
    lower_rows = jnp.concatenate([-imag_part, real_part], axis=-1)
    return jnp.concatenate([upper_rows, lower_rows], axis=1)


def combine(product, k_real, k_imag):
    columns = k_real.shape[-1]
    real_part = product[..., :columns]
    imag_part = product[..., columns:]
    scale_real = k_real[:, :, None, :]
    scale_imag = k_imag[:, :, None, :]
    return jnp.stack(
        [
            scale_real * real_part - scale_imag * imag_part,
            scale_real * imag_part + scale_imag * real_part,
        ],
        axis=2,
    )


def envelope_peak(spectra, row_count):
    groups, freq_total, planes, columns = spectra.shape
    sample_count = min(T_CAP, 2 * freq_total)
    time_block = min(128, sample_count)
    freq_index = jnp.arange(freq_total, dtype=jnp.int32)
    scaling = 1.0 / math.sqrt(freq_total)

    def advance(step_index, running):
        sample_times = step_index * time_block + jnp.arange(time_block, dtype=jnp.int32)
        phase_steps = freq_index[:, None] * sample_times[None, :] % (2 * freq_total)
        angles = phase_steps.astype(jnp.float32) * (math.pi / freq_total)
        cosine = jnp.cos(angles)
        sine_part = jnp.sin(angles)
        twiddle = jnp.stack(
            [jnp.stack([cosine, sine_part], axis=1), jnp.stack([-sine_part, cosine], axis=1)],
            axis=1,
        )
        twiddle_high = lax.optimization_barrier(twiddle.astype(jnp.bfloat16))
        twiddle_low = (twiddle - twiddle_high.astype(jnp.float32)).astype(jnp.bfloat16)
        signal = jnp.einsum(
            "gwcx,wckt->gkxt", spectra, twiddle_high, preferred_element_type=jnp.float32
        )
        signal = signal + jnp.einsum(
            "gwcx,wckt->gkxt", spectra, twiddle_low, preferred_element_type=jnp.float32
        )
        signal = signal * scaling
        magnitude = jnp.sqrt(signal[:, 0] * signal[:, 0] + signal[:, 1] * signal[:, 1])
        magnitude = magnitude.reshape(groups, row_count, columns // row_count, time_block)
        return jnp.maximum(running, jnp.max(magnitude, axis=(1, 3)))

    initial = jnp.zeros((groups, columns // row_count), jnp.float32)
    return lax.fori_loop(0, sample_count // time_block, advance, initial)


def regroup_peaks(moved):
    groups, freq_total, planes, row_count, flaw_count = moved.shape
    return envelope_peak(
        moved.reshape(groups, freq_total, planes, row_count * flaw_count), row_count
    )


def body(
    flaw_cells,
    flaw_blocks,
    element_channel,
    focal_delay,
    beam_field,
    flaw_size,
    flaw_slope,
    noise_level,
):
    freq_count = lax.axis_size("freq")
    freq_total = W_DEV * freq_count
    group_total = flaw_size.shape[0]
    row_total = NB * SB
    first_freq = lax.axis_index("freq") * W_DEV
    angular = (first_freq + jnp.arange(W_DEV, dtype=jnp.int32)).astype(jnp.float32) * (
        math.pi / freq_total
    )
    scan_rows = (
        flaw_blocks.reshape(group_total, NB)[:, :, None] * SB
        + jnp.arange(SB, dtype=jnp.int32)[None, None, :]
    ).reshape(group_total, row_total)
    delays = jnp.moveaxis(
        jnp.take(jnp.take(focal_delay, element_channel, axis=0), scan_rows, axis=1), 0, 2
    )
    fields = jnp.take(beam_field, flaw_cells, axis=3).reshape(
        W_DEV, 2, element_channel.shape[0], group_total, FG
    )
    k_real, k_imag = kirchhoff(angular, flaw_size, flaw_slope)
    focal_terms = focal_law(angular, delays)
    field_terms = field_matrix(fields)
    product = jnp.einsum(
        "wgre,wegf->gwrf", focal_terms, field_terms, preferred_element_type=jnp.float32
    )
    partial_value = combine(product, k_real, k_imag).astype(jnp.bfloat16)
    rounded_term = lax.optimization_barrier(partial_value).astype(jnp.float32)
    summed = lax.psum_scatter(
        rounded_term.astype(jnp.bfloat16), "elem", scatter_dimension=0, tiled=True
    )
    partial_peak = regroup_peaks(
        lax.all_to_all(summed, "freq", split_axis=3, concat_axis=1, tiled=True)
    )
    whole_peak = lax.pmax(partial_peak, "freq")
    columns = FG // freq_count
    flaw_peak = lax.dynamic_slice_in_dim(whole_peak, lax.axis_index("freq") * columns, columns, 1)
    detection = jax.nn.sigmoid(STEEP * (jnp.log(flaw_peak + EPS) - jnp.log(noise_level)))
    return (flaw_peak, detection)


def solution(mesh):
    in_specs = (
        P("batch"),
        P("batch"),
        P("elem"),
        P(),
        P("freq", None, "elem", None),
        P("batch", None),
        P("batch", None),
        P(("batch", "elem"), "freq"),
    )
    out_specs = (P(("batch", "elem"), "freq"), P(("batch", "elem"), "freq"))
    return jax.shard_map(body, mesh=mesh, in_specs=in_specs, out_specs=out_specs, check_vma=False)
```

profile of v0, /device:TPU:0, one launch (start us, length us, event | category | flops | bytes accessed | tf_op | source)
XLA Modules:
  0.0 130.7 jit_solution(10028995258592045228)
XLA Ops:
  7.2 0.0 copy-start
  7.2 0.0 all-reduce.3.cloned.1.call-start
  7.2 0.7 compare_select_fusion.3
  7.9 1.2 compare_and_fusion
  9.1 0.7 broadcast_multiply_fusion.2
  9.7 0.1 mul.298
  9.8 0.1 add.209
  9.9 0.1 add.219
  10.0 0.1 add.210
  10.1 0.7 compare_select_fusion
  10.8 0.7 and_bitcast_fusion
  11.4 3.5 %copy.28 = bf16[16,2,128,256]{2,0,3,1:T(8,128)(2,1)S(1)} copy(bf16[16,2,128,256]{3,2,1,0:T(8,128)(2,1)} %param.14) | data formatting | bytes 4194304 | tf_op args[4]
  14.9 2.3 %gather_fusion.2 = bf16[256,16,2,128]{3,1,2,0:T(8,128)(2,1)} fusion(bf16[16,2,128,256]{2,0,3,1:T(8,128)(2,1)S(1)} %copy.28, s32[1024]{0:T(1024)S(1)} %pad_clamp_fusion), kind=kCustom, calls=%fused_computation.2 | custom fusion | bytes 4195328 | tf_op jit(solution)/shard_map/jit(_take)/gather | solution.py:121
  17.2 3.5 %copy.30 = bf16[16,2,128,2,128]{4,2,0,3,1:T(8,128)(2,1)S(1)} copy(bf16[16,2,128,2,128]{2,0,1,4,3:T(8,128)(2,1)} %bitcast.85) | data formatting | bytes 4194304 | tf_op jit(solution)/shard_map/jit(_take)/gather | solution.py:121
  20.7 0.2 broadcast_select_fusion.1
  20.9 0.1 slice_bitcast_fusion
  21.0 0.1 fusion.42
  21.2 0.1 add.212
  21.3 0.0 copy-done
  21.3 0.8 gather_fusion
  22.1 1.4 %broadcast_select_fusion.3 = f32[128,256]{1,0:T(8,128)} fusion(f32[128,256]{1,0:T(8,128)S(1)} %gather_fusion, pred[128]{0:T(512)(128)(4,1)} %compare_and_fusion), kind=kLoop, calls=%fused_computation.64 | loop fusion | flops 32768 | bytes 262272 | tf_op jit(solution)/shard_map/jit(_take)/select_n | solution.py:119
  23.5 1.0 copy.27
  24.5 0.5 compare_and_fusion.1
  25.0 1.3 %gather_fusion.1 = f32[256,128]{1,0:T(8,128)} fusion(f32[128,256]{0,1:T(8,128)S(1)} %copy.27, s32[1024]{0:T(1024)S(1)} %pad_clamp_fusion.1), kind=kCustom, calls=%fused_computation.1 | custom fusion | bytes 263168 | tf_op jit(solution)/shard_map/jit(_take)/gather | solution.py:119
  26.3 1.0 broadcast_select_fusion.2
  27.3 7.8 %fusion.30 = (bf16[16,2,128,128]{3,2,0,1:T(8,128)(2,1)S(1)}, bf16[16,2,128,128]{3,2,0,1:T(8,128)(2,1)S(1)}) fusion(f32[2,128,128]{2,1,0:T(8,128)S(1)} %broadcast_select_fusion.2, f32[16]{0:T(128)S(1)} %convert_multiply_fusion), kind=kLoop, calls=%fused_computation.49 | loop fusion | flops 2097152 | bytes 2228288 | tf_op jit(solution)/shard_map/convert.4
  35.1 0.7 broadcast_multiply_fusion.1
  35.8 0.1 fusion.38
  36.0 1.4 %fusion.22 = f32[2,16,128,256]{3,2,1,0:T(8,128)S(1)} fusion(bf16[16,128,2,128]{3,1,0,2:T(8,128)(2,1)S(1)} %get-tuple-element.144, bf16[16,128,2,128]{3,1,0,2:T(8,128)(2,1)S(1)} %fusion.42, bf16[16,128,2,128]{3,1,0,2:T(8,128)(2,1)S(1)} %get-tuple-element.143, bf16[16,2,128,128]{3,2,0,1:T(8,128)(2,1)S(1)} %get-tuple-element.146, ...), kind=kOutput, calls=%fused_computation.39 | convolution fusion | flops 557842432 | bytes 9437184 | tf_op jit(solution)/shard_map/wgre,wegf->gwrf/dot_general | solution.py:127
  37.4 0.6 fusion.36
  38.1 1.5 %pad_maximum_fusion.1 = bf16[2,16,2,128,128]{4,3,1,0,2:T(8,128)(2,1)} fusion(bf16[2,16,1,128,128]{4,3,1,0,2:T(8,128)(2,1)S(1)} %get-tuple-element.142, bf16[2,16,1,128,128]{4,3,1,0,2:T(8,128)(2,1)S(1)} %get-tuple-element.141), kind=kLoop, calls=%fused_computation.55 | loop fusion | flops 1048576 | bytes 4194304 | tf_op jit(solution)/shard_map/stack | solution.py:46
  39.5 0.0 copy-start.2
  39.5 0.0 all-reduce.3.cloned.1.call-update
  39.6 0.6 copy-done.2
  40.2 0.6 dynamic-slice
  40.8 22.9 %all-reduce.3.cloned.1.call-done = bf16[2,16,2,128,128]{4,3,1,0,2:T(8,128)(2,1)} async-done(((bf16[2,16,2,128,128]{4,3,1,0,2:T(8,128)(2,1)}), bf16[2,16,2,128,128]{4,3,1,0,2:T(8,128)(2,1)}) %all-reduce.3.cloned.1.call-update) | async-done | bytes 2097168
  63.6 1.9 %constant_dynamic-slice_fusion = bf16[1,16,2,128,128]{4,3,1,0,2:T(8,128)(2,1)S(1)} fusion(bf16[2,16,2,128,128]{4,3,1,0,2:T(8,128)(2,1)} %all-reduce.3.cloned.1.call-done, u32[]{:T(128)} %bitcast.34), kind=kLoop, calls=%fused_computation.81 | loop fusion | bytes 2097156
  65.6 1.7 %copy.31 = bf16[1,16,2,128,128]{4,1,0,2,3:T(8,128)(2,1)} copy(bf16[1,16,2,128,128]{4,3,1,0,2:T(8,128)(2,1)S(1)} %constant_dynamic-slice_fusion) | data formatting | bytes 2097152 | tf_op jit(solution)/shard_map/reduce_scatter | solution.py:132
  67.2 5.8 %all-to-all-start = ((bf16[1,16,2,128,128]{4,1,0,2,3:T(8,128)(2,1)}), bf16[1,16,2,128,128]{4,1,0,2,3:T(8,128)(2,1)S(1)}, u32[]{:S(2)}, u32[]{:S(2)}) async-start(bf16[1,16,2,128,128]{4,1,0,2,3:T(8,128)(2,1)} %copy.31), calls=%async_computation | async-start | bytes 2097152 | tf_op jit(solution)/shard_map/all_to_all | solution.py:136
  73.0 26.2 %all-to-all-done = bf16[1,16,2,128,128]{4,1,0,2,3:T(8,128)(2,1)S(1)} async-done(((bf16[1,16,2,128,128]{4,1,0,2,3:T(8,128)(2,1)}), bf16[1,16,2,128,128]{4,1,0,2,3:T(8,128)(2,1)S(1)}, u32[]{:S(2)}, u32[]{:S(2)}) %all-to-all-start) | async-done | bytes 1048608 | tf_op jit(solution)/shard_map/all_to_all | solution.py:136
  99.2 0.4 copy.32
  99.7 0.5 reshape.333
  100.2 0.0 copy-start.1
  100.2 3.5 %while.16 = (s32[]{:T(128)}, f32[1,128]{1,0:T(1,128)S(1)}, bf16[1,128,2,2048]{3,1,2,0:T(8,128)(2,1)S(1)}, s32[]{:T(128)}, s32[]{:T(128)}, /*index=5*/s32[]{:T(128)}) while((s32[]{:T(128)}, f32[1,128]{1,0:T(1,128)S(1)}, bf16[1,128,2,2048]{3,1,2,0:T(8,128)(2,1)S(1)}, s32[]{:T(128)}, s32[]{:T(128)}, /*index=5*/s32[]{:T(128)}) %tuple.58), condition=%wide.region_4.5_spmd.clone, body=%wide.region_1.4_spmd.clone.sunk | while | flops 539607296 | bytes 12078175 | solution.py:86
  100.2 0.3 fusion.55
  100.6 0.4 convolution_bitcast_fusion.3
  101.0 0.5 fusion.57
  101.5 0.4 fusion.58
  102.0 0.3 fusion.55
  102.4 0.4 convolution_bitcast_fusion.3
  102.8 0.5 fusion.57
  103.3 0.4 fusion.58
  103.7 19.5 %pmax.7 = f32[1,128]{1,0:T(1,128)S(1)} all-reduce(f32[1,128]{1,0:T(1,128)S(1)} %get-tuple-element.113), channel_id=1, replica_groups=mesh['batch'=2,'freq'=8,'elem'=2] {'freq'}, use_global_device_ids=true, to_apply=%region_5.6 | all-reduce | flops 128 | bytes 1024 | tf_op jit(solution)/shard_map/pmax | solution.py:138
  123.2 0.0 copy-done.1
  123.2 0.6 add_divide_fusion
  (17 shorter events, 0.2 us)
Async XLA Ops:
  7.2 14.1 %copy-start = (f32[256,256]{1,0:T(8,128)S(1)}, f32[256,256]{1,0:T(8,128)}, u32[]{:S(2)}) copy-start(f32[256,256]{1,0:T(8,128)} %param.13) | copy-start | bytes 786436
  7.2 56.5 %all-reduce.3.cloned.1.call-start = ((), (), s32[]{:S(2)}) async-start(), calls=%async_computation.1 | async-start | bytes 4194304
  39.5 0.7 copy-start.2
  67.2 32.0 %all-to-all-start = ((bf16[1,16,2,128,128]{4,1,0,2,3:T(8,128)(2,1)}), bf16[1,16,2,128,128]{4,1,0,2,3:T(8,128)(2,1)S(1)}, u32[]{:S(2)}, u32[]{:S(2)}) async-start(bf16[1,16,2,128,128]{4,1,0,2,3:T(8,128)(2,1)} %copy.31), calls=%async_computation | async-start | bytes 2097152 | tf_op jit(solution)/shard_map/all_to_all | solution.py:136
  100.2 23.0 %copy-start.1 = (f32[1,16]{1,0:T(1,128)S(1)}, f32[1,16]{1,0:T(1,128)}, u32[]{:S(2)}) copy-start(f32[1,16]{1,0:T(1,128)} %param.17) | copy-start | bytes 196
Sparse Core Ops, SparseCore 0:
  39.7 23.9 all-reduce.2
where the time goes:
time: 131 us
  waiting for transfers between devices  49.1 us (37%)
  other arithmetic  20.2 us (15%)
  blocking collectives  19.5 us (15%)
  local copies, waits for them, and re-layouts  18.5 us (14%)
  between operations  14.2 us (11%)
  starting transfers between devices  5.81 us (4%)
  matrix products  3.2 us (2%)
    all_to_all x1, waiting for transfers between devices, body(): lax.all_to_all(summed, 'freq', split_axis=3, concat_axis=1, tiled=True)  26.2 us
    unnamed x2, waiting for transfers between devices  22.9 us
    pmax x1, blocking collectives, body(): whole_peak = lax.pmax(partial_peak, 'freq')  19.5 us
    another operation x1, other arithmetic  7.81 us
    unnamed x9, local copies, waits for them, and re-layouts  6.63 us
    all_to_all x1, starting transfers between devices, body(): lax.all_to_all(summed, 'freq', split_axis=3, concat_axis=1, tiled=True)  5.78 us
    gather x2, local copies, waits for them, and re-layouts, body(): jnp.take(beam_field, flaw_cells, axis=3)  5.74 us
  transfers between devices with their start and end apart: 2, of which 2 were waited for; matrix products, arithmetic and copies ran while one was open for 0% of the time, Pallas kernels for 0%

commit v1 on v0

--- a/solution.py
+++ b/solution.py
@@ -1,8 +1,12 @@
+import functools
 import math
 
 import jax
 import jax.numpy as jnp
+import numpy as np
 from jax import lax
+from jax.experimental import pallas as pl
+from jax.experimental.pallas import tpu as pltpu
 from jax.sharding import PartitionSpec as P
 
 W_DEV = 16
@@ -93,7 +97,335 @@
     )
 
 
-def body(
+MESH = pl.DeviceIdType.MESH
+HALF = W_DEV // 2
+TILE_ROWS = 2 * HALF
+NT_DIMS = (((1,), (1,)), ((), ()))
+
+
+def dot_rows(left, right):
+    return lax.dot_general(left, right, NT_DIMS, preferred_element_type=jnp.float32)
+
+
+def unit_phasor(turns):
+    rest = turns - jnp.floor(turns + 0.5)
+    angle = rest * math.pi
+    square = angle * angle
+    sine = jnp.full_like(angle, -1.0 / math.factorial(11))
+    for order, sign in ((9, 1.0), (7, -1.0), (5, 1.0), (3, -1.0), (1, 1.0)):
+        sine = sine * square + sign / math.factorial(order)
+    sine = sine * angle
+    cosine = jnp.full_like(angle, 1.0 / math.factorial(12))
+    for order, sign in ((10, -1.0), (8, 1.0), (6, -1.0), (4, 1.0), (2, -1.0), (0, 1.0)):
+        cosine = cosine * square + sign / math.factorial(order)
+    return 1.0 - 2.0 * sine * sine, -2.0 * sine * cosine
+
+
+def half_twiddles(freq_count):
+    freq_total = W_DEV * freq_count
+    samples = np.arange(freq_total)
+    halves = []
+    for parity in range(2):
+        freqs = (np.arange(freq_count)[:, None] * W_DEV + 2 * np.arange(HALF)[None, :] + parity).reshape(-1)
+        angles = (samples[:, None] * freqs[None, :] % (2 * freq_total)) * (np.pi / freq_total)
+        cosine, sine = np.cos(angles), np.sin(angles)
+        real_rows = np.stack([cosine, -sine], axis=-1).reshape(freq_total, -1)
+        imag_rows = np.stack([sine, cosine], axis=-1).reshape(freq_total, -1)
+        whole = np.concatenate([real_rows, imag_rows], axis=0).astype(np.float32)
+        high = whole.astype(jnp.bfloat16)
+        low = (whole - high.astype(np.float32)).astype(jnp.bfloat16)
+        halves.append(np.concatenate([high, low], axis=1))
+    return np.stack(halves)
+
+
+def inspect_kernel(
+    freq_count,
+    blocks_ref,
+    cells_ref,
+    channel_ref,
+    delay_ref,
+    field_hbm,
+    size_ref,
+    slope_ref,
+    noise_ref,
+    twiddle_ref,
+    peak_ref,
+    detection_ref,
+    field_ref,
+    select_ref,
+    theta_ref,
+    amp_ref,
+    phase_ref,
+    turn_ref,
+    stage_ref,
+    own_ref,
+    give_ref,
+    take_ref,
+    spec_ref,
+    recv_ref,
+    even_ref,
+    top_ref,
+    field_sem,
+    give_sem,
+    take_sem,
+    send_sem,
+    recv_sem,
+):
+    freq_total = W_DEV * freq_count
+    columns = FG // freq_count
+    chunk = columns * TILE_ROWS
+    me = lax.axis_index("freq")
+    mine = lax.axis_index("elem")
+    sibling = 1 - mine
+
+    loads = [
+        pltpu.make_async_copy(field_hbm.at[:, parity], field_ref.at[parity], field_sem.at[parity])
+        for parity in range(2)
+    ]
+    for load in loads:
+        load.start()
+
+    barrier = pltpu.get_barrier_semaphore()
+    pl.semaphore_signal(barrier, inc=1, device_id={"elem": sibling}, device_id_type=MESH)
+    for step in range(1, freq_count):
+        pl.semaphore_signal(
+            barrier, inc=1, device_id={"freq": lax.rem(me + step, freq_count)}, device_id_type=MESH
+        )
+
+    cell_count = cells_ref.shape[1]
+    cell_rows = lax.broadcasted_iota(jnp.int32, (cell_count, cell_count), 0)
+    chosen = jnp.where(cell_rows == cells_ref[...], 1.0, 0.0)
+    select_ref[...] = jnp.transpose(chosen).astype(jnp.bfloat16)
+
+    channel_count, scan_count = delay_ref.shape
+    element_count = channel_ref.shape[1]
+    channel_rows = lax.broadcasted_iota(jnp.int32, (channel_count, element_count), 0)
+    drives = jnp.transpose(jnp.where(channel_rows == channel_ref[...], 1.0, 0.0)).astype(jnp.bfloat16)
+    sub = lax.broadcasted_iota(jnp.int32, (SB, scan_count), 0)
+    lane = lax.broadcasted_iota(jnp.int32, (SB, scan_count), 1)
+    rows = jnp.concatenate(
+        [jnp.where(lane == sub + blocks_ref[j] * SB, 1.0, 0.0) for j in range(2 * NB)], axis=0
+    ).astype(jnp.bfloat16)
+    rest = delay_ref[...]
+    delays = jnp.zeros((2 * FG, element_count), jnp.float32)
+    for _ in range(3):
+        piece = rest.astype(jnp.bfloat16)
+        rest = rest - piece.astype(jnp.float32)
+        by_element = jnp.dot(drives, piece, preferred_element_type=jnp.float32).astype(jnp.bfloat16)
+        delays = delays + dot_rows(rows, by_element)
+    theta_ref[: 2 * FG] = delays
+    for group in range(2):
+        size = jnp.transpose(jnp.broadcast_to(size_ref[group : group + 1, :], (FG, FG)))
+        slope = jnp.transpose(jnp.broadcast_to(slope_ref[group : group + 1, :], (FG, FG)))
+        theta_ref[(2 + group) * FG : (3 + group) * FG] = 2.0 * size * slope
+        amp_ref[group * FG : (group + 1) * FG] = size
+    scale = 0.5 / freq_total
+    turn_real, turn_imag = unit_phasor(theta_ref[...] * (2.0 * scale))
+    turn_ref[0] = turn_real
+    turn_ref[1] = turn_imag
+
+    def group_spectra(parity, group):
+        base = pl.multiple_of(group * FG, FG)
+        tail = pl.multiple_of((2 + group) * FG, FG)
+
+        def one_freq(index, carry):
+            focal_real = phase_ref[0, pl.ds(base, FG), :]
+            focal_imag = phase_ref[1, pl.ds(base, FG), :]
+            fields = dot_rows(select_ref[pl.ds(base, FG), :], field_ref[parity, index])
+            weights = jnp.concatenate(
+                [
+                    jnp.concatenate([focal_real, -focal_imag], axis=1),
+                    jnp.concatenate([focal_imag, focal_real], axis=1),
+                ],
+                axis=0,
+            ).astype(jnp.bfloat16)
+            product = dot_rows(fields.astype(jnp.bfloat16), weights)
+            real_part = product[:, :FG]
+            imag_part = product[:, FG:]
+            edge_real = phase_ref[0, pl.ds(tail, FG), :]
+            edge_imag = phase_ref[1, pl.ds(tail, FG), :]
+            amp = amp_ref[pl.ds(base, FG), :]
+            k_real = amp * (1.0 + EDGE) * edge_real
+            k_imag = amp * (1.0 - EDGE) * edge_imag
+            stage_ref[pl.ds(2 * index, FG, stride=TILE_ROWS), :] = k_real * real_part - k_imag * imag_part
+            stage_ref[pl.ds(2 * index + 1, FG, stride=TILE_ROWS), :] = k_real * imag_part + k_imag * real_part
+            for start, old_real, old_imag in (
+                (base, focal_real, focal_imag),
+                (tail, edge_real, edge_imag),
+            ):
+                step_real = turn_ref[0, pl.ds(start, FG), :]
+                step_imag = turn_ref[1, pl.ds(start, FG), :]
+                phase_ref[0, pl.ds(start, FG), :] = old_real * step_real - old_imag * step_imag
+                phase_ref[1, pl.ds(start, FG), :] = old_real * step_imag + old_imag * step_real
+            return carry
+
+        lax.fori_loop(0, HALF, one_freq, 0)
+
+    pass_copies = [
+        pltpu.make_async_remote_copy(
+            src_ref=give_ref.at[parity],
+            dst_ref=take_ref.at[parity],
+            send_sem=give_sem.at[parity],
+            recv_sem=take_sem.at[parity],
+            device_id={"elem": sibling},
+            device_id_type=MESH,
+        )
+        for parity in range(2)
+    ]
+    order = sorted(range(1, freq_count), key=lambda step: -min(step, freq_count - step))
+    sends = []
+    for parity in range(2):
+        freq_scale = (me * W_DEV + parity).astype(jnp.float32) * scale
+        start_real, start_imag = unit_phasor(theta_ref[...] * freq_scale)
+        phase_ref[0] = start_real
+        phase_ref[1] = start_imag
+        loads[parity].wait()
+        group_spectra(parity, sibling)
+        give_ref[parity] = stage_ref[...].astype(jnp.bfloat16)
+        if parity == 0:
+            pl.semaphore_wait(barrier, freq_count)
+        pass_copies[parity].start()
+        group_spectra(parity, mine)
+        own_ref[...] = stage_ref[...].astype(jnp.bfloat16)
+        pass_copies[parity].wait_recv()
+        total = own_ref[...].astype(jnp.float32) + take_ref[parity].astype(jnp.float32)
+        spec_ref[parity] = total.astype(jnp.bfloat16)
+        for step in order:
+            peer = lax.rem(me + step, freq_count)
+            copy = pltpu.make_async_remote_copy(
+                src_ref=spec_ref.at[parity, pl.ds(pl.multiple_of(peer * chunk, chunk), chunk)],
+                dst_ref=recv_ref.at[parity, me],
+                send_sem=send_sem.at[parity, step],
+                recv_sem=recv_sem.at[parity, me],
+                device_id={"freq": peer},
+                device_id_type=MESH,
+            )
+            copy.start()
+            sends.append(copy)
+        recv_ref[parity, me] = spec_ref[parity, pl.ds(pl.multiple_of(me * chunk, chunk), chunk), :]
+
+    def await_half(parity):
+        for step in order:
+            source = lax.rem(me + step, freq_count)
+            pltpu.make_async_remote_copy(
+                src_ref=spec_ref.at[parity, pl.ds(0, chunk)],
+                dst_ref=recv_ref.at[parity, source],
+                send_sem=send_sem.at[parity, step],
+                recv_sem=recv_sem.at[parity, source],
+                device_id={"freq": source},
+                device_id_type=MESH,
+            ).wait_recv()
+
+    def half_signal(parity, pair):
+        sides = [
+            recv_ref[parity, :, pl.ds(pl.multiple_of((2 * pair + side) * TILE_ROWS, TILE_ROWS), TILE_ROWS), :].reshape(
+                freq_total, FG
+            )
+            for side in range(2)
+        ]
+        both = jnp.concatenate(sides, axis=1)
+        return jnp.dot(
+            twiddle_ref[parity], jnp.concatenate([both, both], axis=0), preferred_element_type=jnp.float32
+        )
+
+    await_half(0)
+
+    def even_pair(pair, carry):
+        even_ref[pair] = half_signal(0, pair)
+        return carry
+
+    lax.fori_loop(0, columns // 2, even_pair, 0)
+    top_ref[...] = jnp.zeros_like(top_ref)
+    await_half(1)
+
+    def odd_pair(pair, carry):
+        odd = half_signal(1, pair)
+        even = even_ref[pair]
+        first = even + odd
+        second = even - odd
+        power = jnp.maximum(
+            first[:freq_total] * first[:freq_total] + first[freq_total:] * first[freq_total:],
+            second[:freq_total] * second[:freq_total] + second[freq_total:] * second[freq_total:],
+        )
+        best = jnp.max(power, axis=0, keepdims=True)
+        top_ref[pl.ds(2 * pair, 1), :] = best[:, :FG]
+        top_ref[pl.ds(2 * pair + 1, 1), :] = best[:, FG:]
+        return carry
+
+    lax.fori_loop(0, columns // 2, odd_pair, 0)
+    strongest = jnp.max(jnp.transpose(top_ref[...]), axis=0, keepdims=True)[:, :columns]
+    flaw_peak = jnp.sqrt(strongest) * (1.0 / math.sqrt(freq_total))
+    peak_ref[...] = flaw_peak
+    level = STEEP * (jnp.log(flaw_peak + EPS) - jnp.log(noise_ref[...]))
+    detection_ref[...] = 1.0 / (1.0 + jnp.exp(-level))
+    for copy in pass_copies:
+        copy.wait_send()
+    for copy in sends:
+        copy.wait_send()
+
+
+def fused_body(
+    flaw_cells,
+    flaw_blocks,
+    element_channel,
+    focal_delay,
+    beam_field,
+    flaw_size,
+    flaw_slope,
+    noise_level,
+):
+    freq_count = lax.axis_size("freq")
+    columns = FG // freq_count
+    elements, cells = beam_field.shape[2:]
+    vmem = pl.BlockSpec(memory_space=pltpu.VMEM)
+    rows = FG * TILE_ROWS
+    chunk = columns * TILE_ROWS
+    freq_total = W_DEV * freq_count
+    out = jax.ShapeDtypeStruct((1, columns), jnp.float32)
+    return pl.pallas_call(
+        functools.partial(inspect_kernel, freq_count),
+        out_shape=(out, out),
+        in_specs=[pl.BlockSpec(memory_space=pltpu.SMEM), vmem, vmem, vmem, pl.BlockSpec(memory_space=pl.ANY)]
+        + [vmem] * 4,
+        out_specs=(vmem, vmem),
+        scratch_shapes=[
+            pltpu.VMEM((2, HALF, 2 * elements, cells), jnp.bfloat16),
+            pltpu.VMEM((cells, cells), jnp.bfloat16),
+            pltpu.VMEM((4 * FG, elements), jnp.float32),
+            pltpu.VMEM((2 * FG, elements), jnp.float32),
+            pltpu.VMEM((2, 4 * FG, elements), jnp.float32),
+            pltpu.VMEM((2, 4 * FG, elements), jnp.float32),
+            pltpu.VMEM((rows, FG), jnp.float32),
+            pltpu.VMEM((rows, FG), jnp.bfloat16),
+            pltpu.VMEM((2, rows, FG), jnp.bfloat16),
+            pltpu.VMEM((2, rows, FG), jnp.bfloat16),
+            pltpu.VMEM((2, rows, FG), jnp.bfloat16),
+            pltpu.VMEM((2, freq_count, chunk, FG), jnp.bfloat16),
+            pltpu.VMEM((columns // 2, 2 * freq_total, 2 * FG), jnp.float32),
+            pltpu.VMEM((FG, FG), jnp.float32),
+            pltpu.SemaphoreType.DMA((2,)),
+            pltpu.SemaphoreType.DMA((2,)),
+            pltpu.SemaphoreType.DMA((2,)),
+            pltpu.SemaphoreType.DMA((2, freq_count)),
+            pltpu.SemaphoreType.DMA((2, freq_count)),
+        ],
+        compiler_params=pltpu.CompilerParams(
+            collective_id=0, has_side_effects=True, vmem_limit_bytes=48 << 20
+        ),
+    )(
+        flaw_blocks,
+        flaw_cells.reshape(1, cells),
+        element_channel.reshape(1, elements),
+        focal_delay,
+        beam_field.reshape(HALF, 2, 2 * elements, cells),
+        flaw_size,
+        flaw_slope,
+        noise_level,
+        jnp.asarray(half_twiddles(freq_count)),
+    )
+
+
+def plain_body(
     flaw_cells,
     flaw_blocks,
     element_channel,
@@ -154,4 +486,8 @@
         P(("batch", "elem"), "freq"),
     )
     out_specs = (P(("batch", "elem"), "freq"), P(("batch", "elem"), "freq"))
+    freq_count = mesh.shape["freq"]
+    freq_total = W_DEV * freq_count
+    whole_tiles = FG % (2 * freq_count) == 0 and freq_total % FG == 0
+    body = fused_body if whole_tiles and 2 * freq_total <= T_CAP else plain_body
     return jax.shard_map(body, mesh=mesh, in_specs=in_specs, out_specs=out_specs, check_vma=False)

time: 131 us -> 45.7 us (0.35)
  waiting for transfers between devices: 49.1 us -> 0 us
  Pallas kernels: 0 us -> 36.2 us
  other arithmetic: 20.2 us -> 0 us
  blocking collectives: 19.5 us -> 0 us
  between operations: 14.2 us -> 0.66 us
  local copies, waits for them, and re-layouts: 18.5 us -> 8.51 us
  starting transfers between devices: 5.81 us -> 0 us
  matrix products: 3.2 us -> 0 us
    pallas_call x0 -> x1, Pallas kernels: none -> 36.2 us  [fused_body(): pl.pallas_call(functools.partial(inspect_kernel, freq_count), out_shape=(...]
    all_to_all x1 -> x0, waiting for transfers between devices: 26.2 us -> none  [body(): lax.all_to_all(summed, 'freq', split_axis=3, concat_axis=1, tiled=True)]
    unnamed x2 -> x0, waiting for transfers between devices: 22.9 us -> none
    pmax x1 -> x0, blocking collectives: 19.5 us -> none  [body(): whole_peak = lax.pmax(partial_peak, 'freq')]
    another operation x5 -> x0, other arithmetic: 9.96 us -> none
    gather x4 -> x0, local copies, waits for them, and re-layouts: 7.83 us -> none  [the longest x2 5.74 us: body(): jnp.take(beam_field, flaw_cells, axis=3)]
    all_to_all x1 -> x0, starting transfers between devices: 5.78 us -> none  [body(): lax.all_to_all(summed, 'freq', split_axis=3, concat_axis=1, tiled=True)]
    select_n x6 -> x0, other arithmetic: 3.99 us -> none  [the longest x2 2.08 us: body(): jnp.take(focal_delay, element_channel, axis=0)]
  transfers between devices with their start and end apart: 2 -> 0, of which waited for: 2 -> 0; matrix products, arithmetic and copies ran while one was open for 0% -> 0% of each run, Pallas kernels for 0% -> 0%
where the time goes in v1:
time: 45.7 us; the launch traced here: 45.4 us
  Pallas kernels  36.2 us (79%)
  local copies, waits for them, and re-layouts  8.51 us (19%)
  between operations  0.66 us (1%)
    pallas_call x1, Pallas kernels, fused_body(): pl.pallas_call(functools.partial(inspect_kernel, freq_count), out_shape=(...  36.2 us
    unnamed x20, local copies, waits for them, and re-layouts  8.51 us

profile of v1, /device:TPU:0, one launch (start us, length us, event | category | flops | bytes accessed | tf_op | source)
XLA Modules:
  0.0 45.4 jit_solution(11236195416975501261)
XLA Ops:
  0.6 0.0 copy-start
  0.6 1.6 %copy-done = bf16[16,2,128,256]{3,2,1,0:T(8,128)(2,1)S(1)} copy-done((bf16[16,2,128,256]{3,2,1,0:T(8,128)(2,1)S(1)}, bf16[16,2,128,256]{3,2,1,0:T(8,128)(2,1)}, u32[]{:S(2)}) %copy-start) | copy-done | bytes 2097176
  2.2 0.0 copy-start.1
  2.2 0.9 %copy-done.1 = f32[256,256]{1,0:T(8,128)S(1)} copy-done((f32[256,256]{1,0:T(8,128)S(1)}, f32[256,256]{1,0:T(8,128)}, u32[]{:S(2)}) %copy-start.1) | copy-done | bytes 262168
  3.2 0.0 copy-start.2
  3.2 0.9 %copy-done.2 = bf16[2,256,256]{2,1,0:T(8,128)(2,1)S(1)} copy-done((bf16[2,256,256]{2,1,0:T(8,128)(2,1)S(1)}, bf16[2,256,256]{2,1,0:T(8,128)(2,1)}, u32[]{:S(2)}) %copy-start.2) | copy-done | bytes 262168
  4.1 0.0 copy-start.3
  4.1 0.7 %copy-done.3 = s32[256]{0:T(256)S(1)} copy-done((s32[256]{0:T(256)S(1)}, s32[256]{0:T(256)}, u32[]{:S(2)}) %copy-start.3) | copy-done | bytes 1048
  4.8 0.0 copy-start.4
  4.8 0.7 %copy-done.4 = f32[2,128]{1,0:T(2,128)S(1)} copy-done((f32[2,128]{1,0:T(2,128)S(1)}, f32[2,128]{1,0:T(2,128)}, u32[]{:S(2)}) %copy-start.4) | copy-done | bytes 1048
  5.5 0.0 copy-start.5
  5.5 0.7 %copy-done.5 = f32[2,128]{1,0:T(2,128)S(1)} copy-done((f32[2,128]{1,0:T(2,128)S(1)}, f32[2,128]{1,0:T(2,128)}, u32[]{:S(2)}) %copy-start.5) | copy-done | bytes 1048
  6.2 0.0 copy-start.6
  6.2 0.7 %copy-done.6 = s32[8]{0:T(128)S(1)} copy-done((s32[8]{0:T(128)S(1)}, s32[8]{0:T(128)}, u32[]{:S(2)}) %copy-start.6) | copy-done | bytes 56
  6.8 0.0 copy-start.7
  6.8 0.7 %copy-done.7 = s32[128]{0:T(128)S(1)} copy-done((s32[128]{0:T(128)S(1)}, s32[128]{0:T(128)}, u32[]{:S(2)}) %copy-start.7) | copy-done | bytes 536
  7.5 0.0 copy-start.8
  7.5 0.7 %copy-done.8 = f32[1,16]{1,0:T(1,128)S(1)} copy-done((f32[1,16]{1,0:T(1,128)S(1)}, f32[1,16]{1,0:T(1,128)}, u32[]{:S(2)}) %copy-start.8) | copy-done | bytes 88
  8.1 36.2 %shard_map.104 = (f32[1,16]{1,0:T(1,128)S(1)}, f32[1,16]{1,0:T(1,128)S(1)}) custom-call(s32[8]{0:T(128)S(1)} %copy-done.6, s32[1,256]{1,0:T(1,128)S(1)} %bitcast.4, s32[1,128]{1,0:T(1,128)S(1)} %bitcast.5, f32[256,256]{1,0:T(8,128)S(1)} %copy-done.1, bf16[8,2,256,256]{3,2,1,0:T(8,128)(2,1)S(1)} %bitcast.3, f32[2,128]{1,0:T(2,128)S(1)} %copy-done.4, ...), custom_call_target="tpu_custom_call" | custom-call | tf_op jit(solution)/shard_map/pallas_call | solution.py:385
  44.4 0.5 %copy.13 = f32[1,16]{1,0:T(1,128)} copy(f32[1,16]{1,0:T(1,128)S(1)} %get-tuple-element.4) | data formatting | bytes 128
  44.9 0.5 %copy.14 = f32[1,16]{1,0:T(1,128)} copy(f32[1,16]{1,0:T(1,128)S(1)} %get-tuple-element.5) | data formatting | bytes 128
Async XLA Ops:
  0.6 1.6 %copy-start = (bf16[16,2,128,256]{3,2,1,0:T(8,128)(2,1)S(1)}, bf16[16,2,128,256]{3,2,1,0:T(8,128)(2,1)}, u32[]{:S(2)}) copy-start(bf16[16,2,128,256]{3,2,1,0:T(8,128)(2,1)} %param.13) | copy-start | bytes 6291460
  2.2 0.9 %copy-start.1 = (f32[256,256]{1,0:T(8,128)S(1)}, f32[256,256]{1,0:T(8,128)}, u32[]{:S(2)}) copy-start(f32[256,256]{1,0:T(8,128)} %delay_ref.1) | copy-start | bytes 786436
  3.2 0.9 %copy-start.2 = (bf16[2,256,256]{2,1,0:T(8,128)(2,1)S(1)}, bf16[2,256,256]{2,1,0:T(8,128)(2,1)}, u32[]{:S(2)}) copy-start(bf16[2,256,256]{2,1,0:T(8,128)(2,1)} %constant.2.clone.twiddle_ref) | copy-start | bytes 786436
  4.1 0.7 %copy-start.3 = (s32[256]{0:T(256)S(1)}, s32[256]{0:T(256)}, u32[]{:S(2)}) copy-start(s32[256]{0:T(256)} %param.9) | copy-start | bytes 3076
  4.8 0.7 %copy-start.4 = (f32[2,128]{1,0:T(2,128)S(1)}, f32[2,128]{1,0:T(2,128)}, u32[]{:S(2)}) copy-start(f32[2,128]{1,0:T(2,128)} %size_ref.1) | copy-start | bytes 3076
  5.5 0.7 %copy-start.5 = (f32[2,128]{1,0:T(2,128)S(1)}, f32[2,128]{1,0:T(2,128)}, u32[]{:S(2)}) copy-start(f32[2,128]{1,0:T(2,128)} %slope_ref.1) | copy-start | bytes 3076
  6.2 0.7 %copy-start.6 = (s32[8]{0:T(128)S(1)}, s32[8]{0:T(128)}, u32[]{:S(2)}) copy-start(s32[8]{0:T(128)} %blocks_ref.1) | copy-start | bytes 100
  6.8 0.7 %copy-start.7 = (s32[128]{0:T(128)S(1)}, s32[128]{0:T(128)}, u32[]{:S(2)}) copy-start(s32[128]{0:T(128)} %param.11) | copy-start | bytes 1540
  7.5 0.7 %copy-start.8 = (f32[1,16]{1,0:T(1,128)S(1)}, f32[1,16]{1,0:T(1,128)}, u32[]{:S(2)}) copy-start(f32[1,16]{1,0:T(1,128)} %noise_ref.1) | copy-start | bytes 196

commit v2 on v1

--- a/solution.py
+++ b/solution.py
@@ -140,17 +140,22 @@
 
 def inspect_kernel(
     freq_count,
+    blocks_hbm,
+    cells_hbm,
+    channel_hbm,
+    delay_hbm,
+    field_hbm,
+    size_hbm,
+    slope_hbm,
+    twiddle_hbm,
+    power_ref,
     blocks_ref,
     cells_ref,
     channel_ref,
     delay_ref,
-    field_hbm,
     size_ref,
     slope_ref,
-    noise_ref,
     twiddle_ref,
-    peak_ref,
-    detection_ref,
     field_ref,
     select_ref,
     theta_ref,
@@ -165,6 +170,7 @@
     recv_ref,
     even_ref,
     top_ref,
+    load_sem,
     field_sem,
     give_sem,
     take_sem,
@@ -178,12 +184,29 @@
     mine = lax.axis_index("elem")
     sibling = 1 - mine
 
+    small = [
+        pltpu.make_async_copy(source, target, load_sem.at[index])
+        for index, (source, target) in enumerate(
+            (
+                (cells_hbm, cells_ref),
+                (channel_hbm, channel_ref),
+                (blocks_hbm, blocks_ref),
+                (delay_hbm, delay_ref),
+                (size_hbm, size_ref),
+                (slope_hbm, slope_ref),
+                (twiddle_hbm, twiddle_ref),
+            )
+        )
+    ]
+    for load in small[:-1]:
+        load.start()
     loads = [
         pltpu.make_async_copy(field_hbm.at[:, parity], field_ref.at[parity], field_sem.at[parity])
         for parity in range(2)
     ]
     for load in loads:
         load.start()
+    small[-1].start()
 
     barrier = pltpu.get_barrier_semaphore()
     pl.semaphore_signal(barrier, inc=1, device_id={"elem": sibling}, device_id_type=MESH)
@@ -192,11 +215,14 @@
             barrier, inc=1, device_id={"freq": lax.rem(me + step, freq_count)}, device_id_type=MESH
         )
 
+    small[0].wait()
     cell_count = cells_ref.shape[1]
     cell_rows = lax.broadcasted_iota(jnp.int32, (cell_count, cell_count), 0)
     chosen = jnp.where(cell_rows == cells_ref[...], 1.0, 0.0)
     select_ref[...] = jnp.transpose(chosen).astype(jnp.bfloat16)
 
+    for load in small[1:-1]:
+        load.wait()
     channel_count, scan_count = delay_ref.shape
     element_count = channel_ref.shape[1]
     channel_rows = lax.broadcasted_iota(jnp.int32, (channel_count, element_count), 0)
@@ -272,7 +298,10 @@
         )
         for parity in range(2)
     ]
-    order = sorted(range(1, freq_count), key=lambda step: -min(step, freq_count - step))
+    half_count = freq_count // 2
+    side = me // half_count
+    peers = [(1 - side) * half_count + lax.rem(me + step, half_count) for step in range(half_count)]
+    peers += [side * half_count + lax.rem(me + step, half_count) for step in range(1, half_count)]
     sends = []
     for parity in range(2):
         freq_scale = (me * W_DEV + parity).astype(jnp.float32) * scale
@@ -290,8 +319,7 @@
         pass_copies[parity].wait_recv()
         total = own_ref[...].astype(jnp.float32) + take_ref[parity].astype(jnp.float32)
         spec_ref[parity] = total.astype(jnp.bfloat16)
-        for step in order:
-            peer = lax.rem(me + step, freq_count)
+        for step, peer in enumerate(peers):
             copy = pltpu.make_async_remote_copy(
                 src_ref=spec_ref.at[parity, pl.ds(pl.multiple_of(peer * chunk, chunk), chunk)],
                 dst_ref=recv_ref.at[parity, me],
@@ -305,8 +333,7 @@
         recv_ref[parity, me] = spec_ref[parity, pl.ds(pl.multiple_of(me * chunk, chunk), chunk), :]
 
     def await_half(parity):
-        for step in order:
-            source = lax.rem(me + step, freq_count)
+        for step, source in enumerate(peers):
             pltpu.make_async_remote_copy(
                 src_ref=spec_ref.at[parity, pl.ds(0, chunk)],
                 dst_ref=recv_ref.at[parity, source],
@@ -328,6 +355,7 @@
             twiddle_ref[parity], jnp.concatenate([both, both], axis=0), preferred_element_type=jnp.float32
         )
 
+    small[-1].wait()
     await_half(0)
 
     def even_pair(pair, carry):
@@ -353,11 +381,7 @@
         return carry
 
     lax.fori_loop(0, columns // 2, odd_pair, 0)
-    strongest = jnp.max(jnp.transpose(top_ref[...]), axis=0, keepdims=True)[:, :columns]
-    flaw_peak = jnp.sqrt(strongest) * (1.0 / math.sqrt(freq_total))
-    peak_ref[...] = flaw_peak
-    level = STEEP * (jnp.log(flaw_peak + EPS) - jnp.log(noise_ref[...]))
-    detection_ref[...] = 1.0 / (1.0 + jnp.exp(-level))
+    power_ref[...] = jnp.max(jnp.transpose(top_ref[...]), axis=0, keepdims=True)
     for copy in pass_copies:
         copy.wait_send()
     for copy in sends:
@@ -381,14 +405,20 @@
     rows = FG * TILE_ROWS
     chunk = columns * TILE_ROWS
     freq_total = W_DEV * freq_count
-    out = jax.ShapeDtypeStruct((1, columns), jnp.float32)
-    return pl.pallas_call(
+    hbm = pl.BlockSpec(memory_space=pltpu.MemorySpace.HBM)
+    power = pl.pallas_call(
         functools.partial(inspect_kernel, freq_count),
-        out_shape=(out, out),
-        in_specs=[pl.BlockSpec(memory_space=pltpu.SMEM), vmem, vmem, vmem, pl.BlockSpec(memory_space=pl.ANY)]
-        + [vmem] * 4,
-        out_specs=(vmem, vmem),
+        out_shape=jax.ShapeDtypeStruct((1, FG), jnp.float32),
+        in_specs=[hbm] * 8,
+        out_specs=vmem,
         scratch_shapes=[
+            pltpu.SMEM(flaw_blocks.shape, jnp.int32),
+            pltpu.VMEM((1, cells), jnp.int32),
+            pltpu.VMEM((1, elements), jnp.int32),
+            pltpu.VMEM(focal_delay.shape, jnp.float32),
+            pltpu.VMEM(flaw_size.shape, jnp.float32),
+            pltpu.VMEM(flaw_slope.shape, jnp.float32),
+            pltpu.VMEM((2, 2 * freq_total, 2 * freq_total), jnp.bfloat16),
             pltpu.VMEM((2, HALF, 2 * elements, cells), jnp.bfloat16),
             pltpu.VMEM((cells, cells), jnp.bfloat16),
             pltpu.VMEM((4 * FG, elements), jnp.float32),
@@ -403,6 +433,7 @@
             pltpu.VMEM((2, freq_count, chunk, FG), jnp.bfloat16),
             pltpu.VMEM((columns // 2, 2 * freq_total, 2 * FG), jnp.float32),
             pltpu.VMEM((FG, FG), jnp.float32),
+            pltpu.SemaphoreType.DMA((7,)),
             pltpu.SemaphoreType.DMA((2,)),
             pltpu.SemaphoreType.DMA((2,)),
             pltpu.SemaphoreType.DMA((2,)),
@@ -410,7 +441,7 @@
             pltpu.SemaphoreType.DMA((2, freq_count)),
         ],
         compiler_params=pltpu.CompilerParams(
-            collective_id=0, has_side_effects=True, vmem_limit_bytes=48 << 20
+            collective_id=0, has_side_effects=True, vmem_limit_bytes=67_043_328
         ),
     )(
         flaw_blocks,
@@ -420,9 +451,11 @@
         beam_field.reshape(HALF, 2, 2 * elements, cells),
         flaw_size,
         flaw_slope,
-        noise_level,
         jnp.asarray(half_twiddles(freq_count)),
     )
+    flaw_peak = jnp.sqrt(power[:, :columns]) * (1.0 / math.sqrt(freq_total))
+    detection = jax.nn.sigmoid(STEEP * (jnp.log(flaw_peak + EPS) - jnp.log(noise_level)))
+    return (flaw_peak, detection)
 
 
 def plain_body(

time: 45.7 us -> 40.9 us (0.89)
  local copies, waits for them, and re-layouts: 8.51 us -> 0 us
  Pallas kernels: 36.2 us -> 38.9 us
  other arithmetic: 0 us -> 1.2 us
    unnamed x20 -> x0, local copies, waits for them, and re-layouts: 8.51 us -> none
    pallas_call x1, Pallas kernels: 36.2 us -> 38.9 us  [fused_body(): pl.pallas_call(functools.partial(inspect_kernel, freq_count), out_shape=j...]
    div x0 -> x1, other arithmetic: none -> 1.2 us  [fused_body(): jax.nn.sigmoid(STEEP * (jnp.log(flaw_peak + EPS) - jnp.log(noise_level)))]
where the time goes in v2:
time: 40.9 us; the launch traced here: 40.7 us
  Pallas kernels  38.9 us (95%)
  other arithmetic  1.2 us (3%)
  between operations  0.64 us (2%)
    pallas_call x1, Pallas kernels, fused_body(): pl.pallas_call(functools.partial(inspect_kernel, freq_count), out_shape=j...  38.9 us
    div x1, other arithmetic, fused_body(): jax.nn.sigmoid(STEEP * (jnp.log(flaw_peak + EPS) - jnp.log(noise_level)))  1.2 us

profile of v2, /device:TPU:0, one launch (start us, length us, event | category | flops | bytes accessed | tf_op | source)
XLA Modules:
  0.0 40.7 jit_solution(4718480542687759487)
XLA Ops:
  0.6 38.9 %shard_map.104 = f32[1,128]{1,0:T(1,128)} custom-call(s32[8]{0:T(128)} %blocks_hbm.1, s32[1,256]{1,0:T(1,128)} %bitcast.4, s32[1,128]{1,0:T(1,128)} %bitcast.5, f32[256,256]{1,0:T(8,128)} %delay_hbm.1, bf16[8,2,256,256]{3,2,1,0:T(8,128)(2,1)} %bitcast.3, f32[2,128]{1,0:T(2,128)} %size_hbm.1, f32[2,128]{1,0:T(2,128)} %slope_hbm.1, ...), custom_call_target="tpu_custom_call" | custom-call | tf_op jit(solution)/shard_map/pallas_call | solution.py:409
  39.5 1.2 %add_divide_fusion = (f32[1,16]{1,0:T(1,128)}, f32[1,16]{1,0:T(1,128)}) fusion(f32[1,16]{1,0:T(1,128)} %param.16, f32[1,128]{1,0:T(1,128)} %shard_map.104), kind=kLoop, calls=%fused_computation | loop fusion | flops 112 | bytes 256 | tf_op jit(solution)/shard_map/div | solution.py:457

commit v3 on v2

--- a/solution.py
+++ b/solution.py
@@ -285,7 +285,7 @@
                 phase_ref[1, pl.ds(start, FG), :] = old_real * step_imag + old_imag * step_real
             return carry
 
-        lax.fori_loop(0, HALF, one_freq, 0)
+        lax.fori_loop(0, HALF, one_freq, 0, unroll=2)
 
     pass_copies = [
         pltpu.make_async_remote_copy(
@@ -380,7 +380,7 @@
         top_ref[pl.ds(2 * pair + 1, 1), :] = best[:, FG:]
         return carry
 
-    lax.fori_loop(0, columns // 2, odd_pair, 0)
+    lax.fori_loop(0, columns // 2, odd_pair, 0, unroll=4 if columns % 8 == 0 else 1)
     power_ref[...] = jnp.max(jnp.transpose(top_ref[...]), axis=0, keepdims=True)
     for copy in pass_copies:
         copy.wait_send()

time: 40.9 us -> 38.3 us (0.936)
  Pallas kernels: 38.9 us -> 36.2 us
    pallas_call x1, Pallas kernels: 38.9 us -> 36.2 us  [fused_body(): pl.pallas_call(functools.partial(inspect_kernel, freq_count), out_shape=j...]
where the time goes in v3:
time: 38.3 us; the launch traced here: 38.1 us
  Pallas kernels  36.2 us (95%)
  other arithmetic  1.2 us (3%)
  between operations  0.64 us (2%)
    pallas_call x1, Pallas kernels, fused_body(): pl.pallas_call(functools.partial(inspect_kernel, freq_count), out_shape=j...  36.2 us
    div x1, other arithmetic, fused_body(): jax.nn.sigmoid(STEEP * (jnp.log(flaw_peak + EPS) - jnp.log(noise_level)))  1.2 us

profile of v3, /device:TPU:0, one launch (start us, length us, event | category | flops | bytes accessed | tf_op | source)
XLA Modules:
  0.0 38.1 jit_solution(10195112827439356235)
XLA Ops:
  0.6 36.2 %shard_map.104 = f32[1,128]{1,0:T(1,128)} custom-call(s32[8]{0:T(128)} %blocks_hbm.1, s32[1,256]{1,0:T(1,128)} %bitcast.4, s32[1,128]{1,0:T(1,128)} %bitcast.5, f32[256,256]{1,0:T(8,128)} %delay_hbm.1, bf16[8,2,256,256]{3,2,1,0:T(8,128)(2,1)} %bitcast.3, f32[2,128]{1,0:T(2,128)} %size_hbm.1, f32[2,128]{1,0:T(2,128)} %slope_hbm.1, ...), custom_call_target="tpu_custom_call" | custom-call | tf_op jit(solution)/shard_map/pallas_call | solution.py:409
  36.9 1.2 %add_divide_fusion = (f32[1,16]{1,0:T(1,128)}, f32[1,16]{1,0:T(1,128)}) fusion(f32[1,16]{1,0:T(1,128)} %param.16, f32[1,128]{1,0:T(1,128)} %shard_map.104), kind=kLoop, calls=%fused_computation | loop fusion | flops 112 | bytes 256 | tf_op jit(solution)/shard_map/div | solution.py:457

commit v4 on v3

--- a/solution.py
+++ b/solution.py
@@ -250,14 +250,15 @@
     turn_ref[0] = turn_real
     turn_ref[1] = turn_imag
 
-    def group_spectra(parity, group):
+    def group_spectra(parity, group, first, count):
         base = pl.multiple_of(group * FG, FG)
-        tail = pl.multiple_of((2 + group) * FG, FG)
+        flaws = pl.multiple_of(group * FG + first, count)
+        tail = pl.multiple_of((2 + group) * FG + first, count)
 
         def one_freq(index, carry):
             focal_real = phase_ref[0, pl.ds(base, FG), :]
             focal_imag = phase_ref[1, pl.ds(base, FG), :]
-            fields = dot_rows(select_ref[pl.ds(base, FG), :], field_ref[parity, index])
+            fields = dot_rows(select_ref[pl.ds(flaws, count), :], field_ref[parity, index])
             weights = jnp.concatenate(
                 [
                     jnp.concatenate([focal_real, -focal_imag], axis=1),
@@ -268,58 +269,68 @@
             product = dot_rows(fields.astype(jnp.bfloat16), weights)
             real_part = product[:, :FG]
             imag_part = product[:, FG:]
-            edge_real = phase_ref[0, pl.ds(tail, FG), :]
-            edge_imag = phase_ref[1, pl.ds(tail, FG), :]
-            amp = amp_ref[pl.ds(base, FG), :]
+            edge_real = phase_ref[0, pl.ds(tail, count), :]
+            edge_imag = phase_ref[1, pl.ds(tail, count), :]
+            amp = amp_ref[pl.ds(flaws, count), :]
             k_real = amp * (1.0 + EDGE) * edge_real
             k_imag = amp * (1.0 - EDGE) * edge_imag
-            stage_ref[pl.ds(2 * index, FG, stride=TILE_ROWS), :] = k_real * real_part - k_imag * imag_part
-            stage_ref[pl.ds(2 * index + 1, FG, stride=TILE_ROWS), :] = k_real * imag_part + k_imag * real_part
-            for start, old_real, old_imag in (
-                (base, focal_real, focal_imag),
-                (tail, edge_real, edge_imag),
+            stage_ref[pl.ds(2 * index, count, stride=TILE_ROWS), :] = k_real * real_part - k_imag * imag_part
+            stage_ref[pl.ds(2 * index + 1, count, stride=TILE_ROWS), :] = k_real * imag_part + k_imag * real_part
+            for start, size, old_real, old_imag in (
+                (base, FG, focal_real, focal_imag),
+                (tail, count, edge_real, edge_imag),
             ):
-                step_real = turn_ref[0, pl.ds(start, FG), :]
-                step_imag = turn_ref[1, pl.ds(start, FG), :]
-                phase_ref[0, pl.ds(start, FG), :] = old_real * step_real - old_imag * step_imag
-                phase_ref[1, pl.ds(start, FG), :] = old_real * step_imag + old_imag * step_real
+                step_real = turn_ref[0, pl.ds(start, size), :]
+                step_imag = turn_ref[1, pl.ds(start, size), :]
+                phase_ref[0, pl.ds(start, size), :] = old_real * step_real - old_imag * step_imag
+                phase_ref[1, pl.ds(start, size), :] = old_real * step_imag + old_imag * step_real
             return carry
 
         lax.fori_loop(0, HALF, one_freq, 0, unroll=2)
 
-    pass_copies = [
-        pltpu.make_async_remote_copy(
-            src_ref=give_ref.at[parity],
-            dst_ref=take_ref.at[parity],
-            send_sem=give_sem.at[parity],
-            recv_sem=take_sem.at[parity],
-            device_id={"elem": sibling},
-            device_id_type=MESH,
-        )
-        for parity in range(2)
-    ]
     half_count = freq_count // 2
     side = me // half_count
     peers = [(1 - side) * half_count + lax.rem(me + step, half_count) for step in range(half_count)]
     peers += [side * half_count + lax.rem(me + step, half_count) for step in range(1, half_count)]
+    far = list(enumerate(peers))[:half_count]
+    near = list(enumerate(peers))[half_count:]
+    half_flaws = FG // 2
+    pieces = (
+        (0, (1 - side) * half_flaws, half_flaws, far, False),
+        (0, side * half_flaws, half_flaws, near, True),
+        (1, 0, FG, far + near, True),
+    )
+    pass_copies = []
     sends = []
-    for parity in range(2):
+    for piece, (parity, first, count, targets, keeps) in enumerate(pieces):
+        size = count * TILE_ROWS
+        span = pl.ds(pl.multiple_of(first * TILE_ROWS, size), size)
         freq_scale = (me * W_DEV + parity).astype(jnp.float32) * scale
         start_real, start_imag = unit_phasor(theta_ref[...] * freq_scale)
         phase_ref[0] = start_real
         phase_ref[1] = start_imag
-        loads[parity].wait()
-        group_spectra(parity, sibling)
-        give_ref[parity] = stage_ref[...].astype(jnp.bfloat16)
-        if parity == 0:
+        if piece != 1:
+            loads[parity].wait()
+        group_spectra(parity, sibling, first, count)
+        give_ref[parity, span, :] = stage_ref[:size].astype(jnp.bfloat16)
+        if piece == 0:
             pl.semaphore_wait(barrier, freq_count)
-        pass_copies[parity].start()
-        group_spectra(parity, mine)
-        own_ref[...] = stage_ref[...].astype(jnp.bfloat16)
-        pass_copies[parity].wait_recv()
-        total = own_ref[...].astype(jnp.float32) + take_ref[parity].astype(jnp.float32)
-        spec_ref[parity] = total.astype(jnp.bfloat16)
-        for step, peer in enumerate(peers):
+        swap = pltpu.make_async_remote_copy(
+            src_ref=give_ref.at[parity, span],
+            dst_ref=take_ref.at[parity, span],
+            send_sem=give_sem.at[piece],
+            recv_sem=take_sem.at[piece],
+            device_id={"elem": sibling},
+            device_id_type=MESH,
+        )
+        swap.start()
+        pass_copies.append(swap)
+        group_spectra(parity, mine, first, count)
+        own_ref[:size] = stage_ref[:size].astype(jnp.bfloat16)
+        swap.wait_recv()
+        total = own_ref[:size].astype(jnp.float32) + take_ref[parity, span, :].astype(jnp.float32)
+        spec_ref[parity, span, :] = total.astype(jnp.bfloat16)
+        for step, peer in targets:
             copy = pltpu.make_async_remote_copy(
                 src_ref=spec_ref.at[parity, pl.ds(pl.multiple_of(peer * chunk, chunk), chunk)],
                 dst_ref=recv_ref.at[parity, me],
@@ -330,7 +341,8 @@
             )
             copy.start()
             sends.append(copy)
-        recv_ref[parity, me] = spec_ref[parity, pl.ds(pl.multiple_of(me * chunk, chunk), chunk), :]
+        if keeps:
+            recv_ref[parity, me] = spec_ref[parity, pl.ds(pl.multiple_of(me * chunk, chunk), chunk), :]
 
     def await_half(parity):
         for step, source in enumerate(peers):
@@ -435,8 +447,8 @@
             pltpu.VMEM((FG, FG), jnp.float32),
             pltpu.SemaphoreType.DMA((7,)),
             pltpu.SemaphoreType.DMA((2,)),
-            pltpu.SemaphoreType.DMA((2,)),
-            pltpu.SemaphoreType.DMA((2,)),
+            pltpu.SemaphoreType.DMA((3,)),
+            pltpu.SemaphoreType.DMA((3,)),
             pltpu.SemaphoreType.DMA((2, freq_count)),
             pltpu.SemaphoreType.DMA((2, freq_count)),
         ],

time: 38.3 us -> 37.6 us (0.982)
  Pallas kernels: 36.2 us -> 35.6 us
    pallas_call x1, Pallas kernels: 36.2 us -> 35.6 us  [fused_body(): pl.pallas_call(functools.partial(inspect_kernel, freq_count), out_shape=j...]
where the time goes in v4:
time: 37.6 us; the launch traced here: 37.5 us
  Pallas kernels  35.6 us (95%)
  other arithmetic  1.2 us (3%)
  between operations  0.64 us (2%)
    pallas_call x1, Pallas kernels, fused_body(): pl.pallas_call(functools.partial(inspect_kernel, freq_count), out_shape=j...  35.6 us
    div x1, other arithmetic, fused_body(): jax.nn.sigmoid(STEEP * (jnp.log(flaw_peak + EPS) - jnp.log(noise_level)))  1.2 us

profile of v4, /device:TPU:0, one launch (start us, length us, event | category | flops | bytes accessed | tf_op | source)
XLA Modules:
  0.0 37.5 jit_solution(17615572406983975020)
XLA Ops:
  0.6 35.6 %shard_map.104 = f32[1,128]{1,0:T(1,128)} custom-call(s32[8]{0:T(128)} %blocks_hbm.1, s32[1,256]{1,0:T(1,128)} %bitcast.4, s32[1,128]{1,0:T(1,128)} %bitcast.5, f32[256,256]{1,0:T(8,128)} %delay_hbm.1, bf16[8,2,256,256]{3,2,1,0:T(8,128)(2,1)} %bitcast.3, f32[2,128]{1,0:T(2,128)} %size_hbm.1, f32[2,128]{1,0:T(2,128)} %slope_hbm.1, ...), custom_call_target="tpu_custom_call" | custom-call | tf_op jit(solution)/shard_map/pallas_call | solution.py:421
  36.2 1.2 %add_divide_fusion = (f32[1,16]{1,0:T(1,128)}, f32[1,16]{1,0:T(1,128)}) fusion(f32[1,16]{1,0:T(1,128)} %param.16, f32[1,128]{1,0:T(1,128)} %shard_map.104), kind=kLoop, calls=%fused_computation | loop fusion | flops 112 | bytes 256 | tf_op jit(solution)/shard_map/div | solution.py:469
